TPU v7x, 32 devices: a whole 2x2x4 slice. The times are simulated.
32 devices in a mesh: dp: 8 (over z, core), mp: 4 (over y, x).
Axes of the slice: x: 2, y: 2, z: 4, core: 2. Of those that a mesh axis runs over, the one named last changes fastest.
Arguments:
- tokens: bfloat16 [12288, 2048], P(('dp', 'mp')), may hold values from -6 to 6
- segment_ids: int32 [16, 768], P('dp'), may hold values from 0 to 5, never falling along the last dimension, each value on 1 to 256 neighbouring positions
- query_weight: bfloat16 [2048, 2048], P(None, 'mp'), may hold values from -0.125 to 0.125
- key_weight: bfloat16 [2048, 2048], P(None, 'mp'), may hold values from -0.125 to 0.125
- value_weight: bfloat16 [2048, 2048], P(None, 'mp'), may hold values from -0.125 to 0.125
- out_weight: bfloat16 [2048, 2048], P('mp'), may hold values from -0.75 to 0.75
- up_weight: bfloat16 [2048, 8192], P(None, 'mp'), may hold values from -0.125 to 0.125
- down_weight: bfloat16 [8192, 2048], P('mp'), may hold values from -0.0625 to 0.0625
- attn_gain: float32 [2048], replicated, may hold values from 0.5 to 1.5
- mlp_gain: float32 [2048], replicated, may hold values from 0.5 to 1.5
- out_cotangent: bfloat16 [12288, 2048], P(('dp', 'mp')), may hold values from -18 to 18
Outputs:
- layer_output: bfloat16 [12288, 2048], P(('dp', 'mp'))
- tokens_grad: float32 [12288, 2048], P(('dp', 'mp'))
- query_weight_grad: float32 [2048, 2048], P('dp', 'mp')
- key_weight_grad: float32 [2048, 2048], P('dp', 'mp')
- value_weight_grad: float32 [2048, 2048], P('dp', 'mp')
- out_weight_grad: float32 [2048, 2048], P('mp', 'dp')
- up_weight_grad: float32 [2048, 8192], P('dp', 'mp')
- down_weight_grad: float32 [8192, 2048], P('mp', 'dp')
- attn_gain_grad: float32 [2048], replicated
- mlp_gain_grad: float32 [2048], replicated
Inputs may be any that keep to these rules, and one draw needn't show every extreme that they name: `segment_ids`: within each packed sequence the clip numbers never fall; each clip covers 1 to 256 tokens, and some clip covers exactly 256.
All inputs are finite; a program needn't handle non-finite values.
Results may differ from a plain program's by a relative error of at most 0.02.
Values may be sent and summed in bfloat16 or wider, within the bound.
A program may use at most 192 MiB of HBM per device.

v0:
```python
import math
import jax
import jax.numpy as jnp
from jax import lax
from jax.sharding import PartitionSpec as P

HEAD_DIM = 128
epsilon = 1e-05
masked_score = -1e30


def norm_rows(values, gain):
    centre = jnp.mean(values, axis=-1, keepdims=True)
    centred = values - centre
    spread = jnp.mean(centred * centred, axis=-1, keepdims=True)
    return centred * lax.rsqrt(spread + epsilon) * gain


def gelu_tanh(values):
    return jax.nn.gelu(values, approximate=True)


def block_allowed(segment):
    position = jnp.arange(segment.shape[0])
    return (position[None, :] <= position[:, None]) & (segment[:, None] == segment[None, :])


def rows_times(left_rows, right_matrix):
    return jnp.dot(left_rows, right_matrix, preferred_element_type=jnp.float32)


def rows_times_back(left_rows, right_matrix):
    return lax.dot_general(
        left_rows, right_matrix, (((1,), (1,)), ((), ())), preferred_element_type=jnp.float32
    )


def attn_input_back(
    queries_grad, keys_grad, values_grad, query_weight, key_weight, value_weight, score_scale
):
    total_grad = rows_times_back(queries_grad, query_weight) * score_scale
    total_grad = total_grad + rows_times_back(keys_grad, key_weight)
    return total_grad + rows_times_back(values_grad, value_weight)


def attend_forward(packed):
    queries, keys_in, values_in, segment = packed
    scores = jnp.einsum("qhd,khd->hqk", queries, keys_in, preferred_element_type=jnp.float32)
    scores = jnp.where(block_allowed(segment)[None], scores, masked_score)
    row_max = jnp.max(scores, axis=-1, keepdims=True)
    expanded = jnp.exp(scores - row_max)
    row_total = jnp.sum(expanded, axis=-1, keepdims=True)
    probs_low = (expanded / row_total).astype(jnp.bfloat16)
    context = jnp.einsum("hqk,khd->qhd", probs_low, values_in, preferred_element_type=jnp.float32)
    return (context.astype(jnp.bfloat16), (row_max + jnp.log(row_total))[:, :, 0])


def attend_backward(packed):
    queries, keys_in, values_in, segment, context_grad, log_total = packed
    scores = jnp.einsum("qhd,khd->hqk", queries, keys_in, preferred_element_type=jnp.float32)
    scores = jnp.where(block_allowed(segment)[None], scores, masked_score)
    attn_probs = jnp.exp(scores - log_total[:, :, None])
    probs_grad = jnp.einsum(
        "qhd,khd->hqk", context_grad, values_in, preferred_element_type=jnp.float32
    )
    values_grad = jnp.einsum(
        "hqk,qhd->khd",
        attn_probs.astype(jnp.bfloat16),
        context_grad,
        preferred_element_type=jnp.float32,
    )
    inner_sum = jnp.sum(attn_probs * probs_grad, axis=-1, keepdims=True)
    scores_grad = (attn_probs * (probs_grad - inner_sum)).astype(jnp.bfloat16)
    queries_grad = jnp.einsum(
        "hqk,khd->qhd", scores_grad, keys_in, preferred_element_type=jnp.float32
    )
    keys_grad = jnp.einsum("hqk,qhd->khd", scores_grad, queries, preferred_element_type=jnp.float32)
    return (
        queries_grad.astype(jnp.bfloat16),
        keys_grad.astype(jnp.bfloat16),
        values_grad.astype(jnp.bfloat16),
    )


def local(
    tokens,
    segment_ids,
    query_weight,
    key_weight,
    value_weight,
    out_weight,
    up_weight,
    down_weight,
    attn_gain,
    mlp_gain,
    out_cotangent,
):
    seq_count, seq_length = segment_ids.shape
    group_rows = seq_count * seq_length
    head_count = query_weight.shape[1] // HEAD_DIM
    score_scale = 1.0 / math.sqrt(HEAD_DIM)
    shaped = (seq_count, seq_length, head_count, HEAD_DIM)
    flat_shape = (group_rows, head_count * HEAD_DIM)
    residual_in = tokens.astype(jnp.float32)
    normed_attn, attn_norm_back = jax.vjp(norm_rows, residual_in, attn_gain)
    gathered_attn = lax.all_gather(normed_attn.astype(jnp.bfloat16), "mp", axis=0, tiled=True)
    queries = (
        jnp.dot(gathered_attn, query_weight, preferred_element_type=jnp.float32) * score_scale
    ).astype(jnp.bfloat16)
    keys_all = jnp.dot(gathered_attn, key_weight, preferred_element_type=jnp.float32).astype(
        jnp.bfloat16
    )
    values_all = jnp.dot(gathered_attn, value_weight, preferred_element_type=jnp.float32).astype(
        jnp.bfloat16
    )
    queries_seq = queries.reshape(shaped)
    keys_seq = keys_all.reshape(shaped)
    values_seq = values_all.reshape(shaped)
    context, log_total = lax.map(attend_forward, (queries_seq, keys_seq, values_seq, segment_ids))
    context_flat = context.reshape(flat_shape)
    attn_rows = lax.psum_scatter(
        rows_times(context_flat, out_weight).astype(jnp.bfloat16),
        "mp",
        scatter_dimension=0,
        tiled=True,
    ).astype(jnp.float32)
    residual_mid = residual_in + attn_rows
    normed_mlp, mlp_norm_back = jax.vjp(norm_rows, residual_mid, mlp_gain)
    gathered_mlp = lax.all_gather(normed_mlp.astype(jnp.bfloat16), "mp", axis=0, tiled=True)
    pre_act = jnp.dot(gathered_mlp, up_weight, preferred_element_type=jnp.float32)
    activated, gelu_back = jax.vjp(gelu_tanh, pre_act)
    hidden = activated.astype(jnp.bfloat16)
    mlp_rows = lax.psum_scatter(
        rows_times(hidden, down_weight).astype(jnp.bfloat16), "mp", scatter_dimension=0, tiled=True
    ).astype(jnp.float32)
    layer_output = (residual_mid + mlp_rows).astype(jnp.bfloat16)
    cotangent_all = lax.all_gather(out_cotangent, "mp", axis=0, tiled=True)
    down_weight_grad = jnp.einsum(
        "rf,rd->fd", hidden, cotangent_all, preferred_element_type=jnp.float32
    )
    hidden_grad = lax.dot_general(
        cotangent_all, down_weight, (((1,), (1,)), ((), ())), preferred_element_type=jnp.float32
    )
    pre_grad = gelu_back(hidden_grad)[0].astype(jnp.bfloat16)
    up_weight_grad = jnp.einsum(
        "rd,rf->df", gathered_mlp, pre_grad, preferred_element_type=jnp.float32
    )
    normed_mlp_grad = lax.psum_scatter(
        rows_times_back(pre_grad, up_weight).astype(jnp.bfloat16),
        "mp",
        scatter_dimension=0,
        tiled=True,
    ).astype(jnp.float32)
    middle_back, mlp_gain_grad = mlp_norm_back(normed_mlp_grad)
    middle_grad = out_cotangent.astype(jnp.float32) + middle_back
    middle_all_grad = lax.all_gather(middle_grad.astype(jnp.bfloat16), "mp", axis=0, tiled=True)
    out_weight_grad = jnp.einsum(
        "rc,rd->cd", context_flat, middle_all_grad, preferred_element_type=jnp.float32
    )
    context_grad = lax.dot_general(
        middle_all_grad, out_weight, (((1,), (1,)), ((), ())), preferred_element_type=jnp.float32
    ).astype(jnp.bfloat16)
    queries_grad, keys_grad, values_grad = lax.map(
        attend_backward,
        (queries_seq, keys_seq, values_seq, segment_ids, context_grad.reshape(shaped), log_total),
    )
    queries_grad = queries_grad.reshape(flat_shape)
    keys_grad = keys_grad.reshape(flat_shape)
    values_grad = values_grad.reshape(flat_shape)
    query_weight_grad = (
        jnp.einsum("rd,rc->dc", gathered_attn, queries_grad, preferred_element_type=jnp.float32)
        * score_scale
    )
    key_weight_grad = jnp.einsum(
        "rd,rc->dc", gathered_attn, keys_grad, preferred_element_type=jnp.float32
    )
    value_weight_grad = jnp.einsum(
        "rd,rc->dc", gathered_attn, values_grad, preferred_element_type=jnp.float32
    )
    normed_attn_grad = lax.psum_scatter(
        attn_input_back(
            queries_grad,
            keys_grad,
            values_grad,
            query_weight,
            key_weight,
            value_weight,
            score_scale,
        ).astype(jnp.bfloat16),
        "mp",
        scatter_dimension=0,
        tiled=True,
    ).astype(jnp.float32)
    token_back, attn_gain_grad = attn_norm_back(normed_attn_grad)
    tokens_grad = middle_grad + token_back
    attn_gain_grad, mlp_gain_grad = lax.psum((attn_gain_grad, mlp_gain_grad), ("dp", "mp"))
    (
        query_weight_grad,
        key_weight_grad,
        value_weight_grad,
        out_weight_grad,
        up_weight_grad,
        down_weight_grad,
    ) = (
        lax.psum_scatter(
            query_weight_grad.astype(jnp.bfloat16), "dp", scatter_dimension=0, tiled=True
        ).astype(jnp.float32),
        lax.psum_scatter(
            key_weight_grad.astype(jnp.bfloat16), "dp", scatter_dimension=0, tiled=True
        ).astype(jnp.float32),
        lax.psum_scatter(
            value_weight_grad.astype(jnp.bfloat16), "dp", scatter_dimension=0, tiled=True
        ).astype(jnp.float32),
        lax.psum_scatter(
            out_weight_grad.astype(jnp.bfloat16), "dp", scatter_dimension=1, tiled=True
        ).astype(jnp.float32),
        lax.psum_scatter(
            up_weight_grad.astype(jnp.bfloat16), "dp", scatter_dimension=0, tiled=True
        ).astype(jnp.float32),
        lax.psum_scatter(
            down_weight_grad.astype(jnp.bfloat16), "dp", scatter_dimension=1, tiled=True
        ).astype(jnp.float32),
    )
    return (
        layer_output,
        tokens_grad,
        query_weight_grad,
        key_weight_grad,
        value_weight_grad,
        out_weight_grad,
        up_weight_grad,
        down_weight_grad,
        attn_gain_grad,
        mlp_gain_grad,
    )


def solution(mesh):
    return jax.shard_map(
        local,
        mesh=mesh,
        in_specs=(
            P(("dp", "mp"), None),
            P("dp", None),
            P(None, "mp"),
            P(None, "mp"),
            P(None, "mp"),
            P("mp", None),
            P(None, "mp"),
            P("mp", None),
            P(),
            P(),
            P(("dp", "mp"), None),
        ),
        out_specs=(
            P(("dp", "mp"), None),
            P(("dp", "mp"), None),
            P("dp", "mp"),
            P("dp", "mp"),
            P("dp", "mp"),
            P("mp", "dp"),
            P("dp", "mp"),
            P("mp", "dp"),
            P(),
            P(),
        ),
        check_vma=False,
    )
```

profile of v0, /device:TPU:0, one launch (start us, length us, event | category | flops | bytes accessed | tf_op | source)
XLA Modules:
  0.0 1105.6 jit_solution(7210589673843302547)
XLA Ops:
  14.0 73.0 %all-gather.5.cloned.1.call-done = bf16[1536,2048]{1,0:T(8,128)(2,1)} async-done(((bf16[384,2048]{1,0:T(8,128)(2,1)}), bf16[1536,2048]{1,0:T(8,128)(2,1)}) %all-gather.5.cloned.1.call-update) | async-done | bytes 6291472 | tf_op jit(solution)/shard_map/all_gather | solution.py:106
  87.0 8.0 convolution_convert_fusion.11
  127.6 28.2 %while.26 = (s32[]{:T(128)}, bf16[2,768,4,128]{3,2,1,0:T(4,128)(2,1)}, f32[2,4,768]{2,1,0:T(4,128)S(1)}, bf16[2,768,4,128]{3,2,1,0:T(4,128)(2,1)}, s32[2,768]{1,...) while((s32[]{:T(128)}, ...), condition=%wide.region_5.6_spmd, body=%wide.region_2.5_spmd.sunk | while | flops 1231352832 | bytes 43362440 | solution.py:119
  163.8 69.6 %reduce-scatter.11.cloned.1.call-done = bf16[384,2048]{1,0:T(8,128)(2,1)} async-done(((bf16[1536,2048]{1,0:T(8,128)(2,1)}), bf16[384,2048]{1,0:T(8,128)(2,1)}) %reduce-scatter.11.cloned.1.call-update) | async-done | bytes 1572880 | tf_op jit(solution)/shard_map/reduce_scatter | solution.py:121
  238.9 66.6 %all-gather.9.cloned.1.call-done = bf16[1536,2048]{1,0:T(8,128)(2,1)} async-done(((bf16[384,2048]{1,0:T(8,128)(2,1)}), bf16[1536,2048]{1,0:T(8,128)(2,1)}) %all-gather.9.cloned.1.call-update) | async-done | bytes 6291472 | tf_op jit(solution)/shard_map/all_gather | solution.py:137
  305.5 19.1 %fusion.89 = f32[1536,2048]{1,0:T(8,128)} fusion(bf16[1536,2048]{1,0:T(8,128)(2,1)} %all-gather.9.cloned.1.call-done, bf16[2048,2048]{1,0:T(8,128)(2,1)} %param.22), kind=kOutput, calls=%fused_computation.146 | convolution fusion | flops 12884901888 | bytes 27262976 | tf_op jit(solution)/shard_map/dot_general | solution.py:141
  324.5 53.4 %all-gather.7.cloned.1.call-done = bf16[1536,2048]{1,0:T(8,128)(2,1)} async-done(((bf16[384,2048]{1,0:T(8,128)(2,1)}), bf16[1536,2048]{1,0:T(8,128)(2,1)}) %all-gather.7.cloned.1.call-update) | async-done | bytes 6291472 | tf_op jit(solution)/shard_map/all_gather | solution.py:129
  377.9 29.6 %fusion.48 = (bf16[1536,2048]{1,0:T(8,128)(2,1)}, f32[1536,2048]{1,0:T(8,128)}) fusion(f32[1536,2048]{1,0:T(8,128)} %fusion.89, bf16[1536,2048]{1,0:T(8,128)(2,1)} %all-gather.7.cloned.1.call-done, bf16[2048,2048]{1,0:T(8,128)(2,1)} %param.21), kind=kOutput, calls=%fused_computation.68 | convolution fusion | flops 12947816448 | bytes 46137344 | tf_op jit(solution)/shard_map/dot_general | solution.py:130
  407.5 19.1 %convolution_convert_fusion.4 = bf16[1536,2048]{1,0:T(8,128)(2,1)} fusion(bf16[1536,2048]{1,0:T(8,128)(2,1)} %get-tuple-element.190, bf16[2048,2048]{1,0:T(8,128)(2,1)} %param.21), kind=kOutput, calls=%fused_computation.73 | convolution fusion | flops 12888047616 | bytes 20971520 | tf_op jit(solution)/shard_map/dot_general | solution.py:33
  426.7 20.5 %convolution_convert_fusion.5 = bf16[1536,2048]{1,0:T(8,128)(2,1)} fusion(bf16[2048,2048]{1,0:T(8,128)(2,1)} %param.22, f32[1536,2048]{1,0:T(8,128)} %get-tuple-element.191), kind=kOutput, calls=%fused_computation.74 | convolution fusion | flops 12916359168 | bytes 27262976 | tf_op jit(solution)/shard_map/dot_general | solution.py:29
  447.3 49.7 %reduce-scatter.15.cloned.1.call-done = bf16[384,2048]{1,0:T(8,128)(2,1)} async-done(((bf16[1536,2048]{1,0:T(8,128)(2,1)}), bf16[384,2048]{1,0:T(8,128)(2,1)}) %reduce-scatter.15.cloned.1.call-update) | async-done | bytes 1572880 | tf_op jit(solution)/shard_map/reduce_scatter | solution.py:148
  501.4 68.7 %reduce-scatter.13.cloned.1.call-done = bf16[384,2048]{1,0:T(8,128)(2,1)} async-done(((bf16[1536,2048]{1,0:T(8,128)(2,1)}), bf16[384,2048]{1,0:T(8,128)(2,1)}) %reduce-scatter.13.cloned.1.call-update) | async-done | bytes 1572880 | tf_op jit(solution)/shard_map/reduce_scatter | solution.py:133
  578.9 19.6 %convolution_convert_fusion.3 = bf16[2048,2048]{1,0:T(8,128)(2,1)} fusion(bf16[1536,2048]{1,0:T(8,128)(2,1)} %all-gather.7.cloned.1.call-done, bf16[1536,2048]{1,0:T(8,128)(2,1)} %get-tuple-element.190), kind=kOutput, calls=%fused_computation.72 | convolution fusion | flops 12889096192 | bytes 20971520 | tf_op jit(solution)/shard_map/rd,rf->df/dot_general | solution.py:145
  598.5 22.5 %convolution_convert_fusion.2 = bf16[2048,2048]{1,0:T(8,128)(2,1)} fusion(bf16[1536,2048]{1,0:T(8,128)(2,1)} %all-gather.9.cloned.1.call-done, f32[1536,2048]{1,0:T(8,128)} %get-tuple-element.191), kind=kOutput, calls=%fused_computation.71 | convolution fusion | flops 12917407744 | bytes 27262976 | tf_op jit(solution)/shard_map/rf,rd->fd/dot_general | solution.py:138
  621.1 28.0 %all-gather.11.cloned.1.call-done = bf16[1536,2048]{1,0:T(8,128)(2,1)} async-done(((bf16[384,2048]{1,0:T(8,128)(2,1)}), bf16[1536,2048]{1,0:T(8,128)(2,1)}) %all-gather.11.cloned.1.call-update) | async-done | bytes 6291472 | tf_op jit(solution)/shard_map/all_gather | solution.py:156
  660.6 8.1 convolution_convert_fusion.7
  673.6 99.9 %while.27 = (s32[]{:T(128)}, bf16[2,768,4,128]{3,2,1,0:T(4,128)(2,1)}, bf16[2,768,4,128]{3,2,1,0:T(4,128)(2,1)}, bf16[2,768,4,128]{3,2,1,0:T(4,128)(2,1)}, bf16[...) while((s32[]{:T(128)}, ...), condition=%wide.region_15.16_spmd, body=%wide.region_13.15_spmd.sunk | while | flops 3051156480 | bytes 169179440 | solution.py:163
  689.0 8.2 multiply_reduce_fusion.3
  697.2 10.9 multiply_convert_fusion.7
  738.5 8.1 multiply_reduce_fusion.3
  746.6 11.5 %multiply_convert_fusion.7 = bf16[4,768,768]{1,2,0:T(8,128)(2,1)} fusion(f32[4,768,768]{1,2,0:T(8,128)} %get-tuple-element.304, f32[4,768,768]{1,2,0:T(8,128)} %copy-done.1, f32[4,768]{1,0:T(4,128)S(1)} %get-tuple-element.305, f32[4,768]{1,0:T(4,128)S(1)} %dynamic-slice_bitcast_fusion.2, pred[768,768]{0,1:T(8,128)(4,1)S(1)} %fusion.146), kind=kLoop, calls=%fused_computation.21.clone.1 | loop fusion | flops 11796480 | bytes 24207360 | tf_op jit(solution)/shard_map/while/body/eval_jaxpr/convert_element_type | solution.py:73
  773.5 8.1 multiply_convert_fusion.2
  781.7 8.1 convolution_convert_fusion.8
  789.8 8.1 convolution_convert_fusion.9
  798.3 10.2 fusion.72
  815.0 15.8 %add_convert_fusion = bf16[1536,2048]{1,0:T(8,128)(2,1)} fusion(f32[1536,2048]{1,0:T(8,128)} %fusion.69, f32[1536,2048]{1,0:T(8,128)} %fusion.72, bf16[2048,512]{1,0:T(8,128)(2,1)} %param.17, bf16[192,8,4,128]{3,2,1,0:T(4,128)(2,1)} %bitcast.147), kind=kOutput, calls=%fused_computation.69 | convolution fusion | flops 3233808384 | bytes 35127296 | tf_op jit(solution)/shard_map/dot_general | solution.py:33
  836.4 31.3 %reduce-scatter.25.cloned.1.call-done = bf16[512,256]{1,0:T(8,128)(2,1)} async-done(((bf16[512,2048]{1,0:T(8,128)(2,1)}), bf16[512,256]{1,0:T(8,128)(2,1)}) %reduce-scatter.25.cloned.1.call-update) | async-done | bytes 262160 | tf_op jit(solution)/shard_map/reduce_scatter | solution.py:214
  869.4 34.9 %reduce-scatter.19.cloned.1.call-done = bf16[256,512]{1,0:T(8,128)(2,1)} async-done(((bf16[2048,512]{1,0:T(8,128)(2,1)}), bf16[256,512]{1,0:T(8,128)(2,1)}) %reduce-scatter.19.cloned.1.call-update) | async-done | bytes 262160 | tf_op jit(solution)/shard_map/reduce_scatter | solution.py:205
  906.1 34.9 %reduce-scatter.23.cloned.1.call-done = bf16[256,512]{1,0:T(8,128)(2,1)} async-done(((bf16[2048,512]{1,0:T(8,128)(2,1)}), bf16[256,512]{1,0:T(8,128)(2,1)}) %reduce-scatter.23.cloned.1.call-update) | async-done | bytes 262160 | tf_op jit(solution)/shard_map/reduce_scatter | solution.py:211
  942.9 34.9 %reduce-scatter.21.cloned.1.call-done = bf16[256,512]{1,0:T(8,128)(2,1)} async-done(((bf16[2048,512]{1,0:T(8,128)(2,1)}), bf16[256,512]{1,0:T(8,128)(2,1)}) %reduce-scatter.21.cloned.1.call-update) | async-done | bytes 262160 | tf_op jit(solution)/shard_map/reduce_scatter | solution.py:208
  979.6 70.0 %reduce-scatter.17.cloned.1.call-done = bf16[384,2048]{1,0:T(8,128)(2,1)} async-done(((bf16[1536,2048]{1,0:T(8,128)(2,1)}), bf16[384,2048]{1,0:T(8,128)(2,1)}) %reduce-scatter.17.cloned.1.call-update) | async-done | bytes 1572880 | tf_op jit(solution)/shard_map/reduce_scatter | solution.py:180
  1054.0 39.5 %all-reduce = (f32[2048]{0:T(1024)}, f32[2048]{0:T(1024)}) all-reduce(f32[2048]{0:T(1024)S(1)} %get-tuple-element.143, f32[2048]{0:T(1024)S(1)} %copy-done.27), channel_id=1, replica_groups=mesh['dp'=8,'mp'=4] {'dp','mp'}, use_global_device_ids=true, to_apply=%region_26.27 | all-reduce | flops 4096 | bytes 32768 | tf_op jit(solution)/shard_map/psum | solution.py:196
  (200 shorter events, 200.6 us)
Async XLA Ops:
  7.2 148.6 %copy-start = (bf16[512,2048]{1,0:T(8,128)(2,1)S(1)}, bf16[512,2048]{1,0:T(8,128)(2,1)}, u32[]{:S(2)}) copy-start(bf16[512,2048]{1,0:T(8,128)(2,1)} %param.20) | copy-start | bytes 6291460
  7.2 5.0 copy-start.20
  7.2 79.8 %all-gather.5.cloned.1.call-start = ((), (), s32[]{:S(2)}) async-start(), calls=%async_computation.10 | async-start | bytes 7864320 | tf_op jit(solution)/shard_map/all_gather | solution.py:106
  7.2 5.0 copy-start.3
  13.9 219.5 %reduce-scatter.11.cloned.1.call-start = ((), (), s32[]{:S(2)}) async-start(), calls=%async_computation.11 | async-start | bytes 7864320 | tf_op jit(solution)/shard_map/reduce_scatter | solution.py:121
  122.6 5.1 copy-start.18
  155.8 7.2 copy-start.16
  163.1 142.4 %all-gather.9.cloned.1.call-start = ((), (), s32[]{:S(2)}) async-start(), calls=%async_computation.14 | async-start | bytes 7864320 | tf_op jit(solution)/shard_map/all_gather | solution.py:137
  163.1 73.9 %copy-start.24 = (f32[2048]{0:T(1024)S(1)}, f32[2048]{0:T(1024)}, u32[]{:S(2)}) copy-start(f32[2048]{0:T(1024)} %param.24) | copy-start | bytes 24580
  163.8 214.1 %all-gather.7.cloned.1.call-start = ((), (), s32[]{:S(2)}) async-start(), calls=%async_computation.12 | async-start | bytes 7864320 | tf_op jit(solution)/shard_map/all_gather | solution.py:129
  238.8 258.2 %reduce-scatter.15.cloned.1.call-start = ((), (), s32[]{:S(2)}) async-start(), calls=%async_computation.15 | async-start | bytes 7864320 | tf_op jit(solution)/shard_map/reduce_scatter | solution.py:148
  426.7 143.4 %reduce-scatter.13.cloned.1.call-start = ((), (), s32[]{:S(2)}) async-start(), calls=%async_computation.13 | async-start | bytes 7864320 | tf_op jit(solution)/shard_map/reduce_scatter | solution.py:133
  447.2 201.9 %all-gather.11.cloned.1.call-start = ((), (), s32[]{:S(2)}) async-start(), calls=%async_computation.16 | async-start | bytes 7864320 | tf_op jit(solution)/shard_map/all_gather | solution.py:156
  570.1 7.2 copy-start.13
  578.8 252.0 %reduce-scatter.27.cloned.1.call-start = ((), (), s32[]{:S(2)}) async-start(), calls=%async_computation.22 | async-start | bytes 9437184 | tf_op jit(solution)/shard_map/reduce_scatter | solution.py:217
  598.5 235.2 %reduce-scatter.29.cloned.1.call-start = ((), (), s32[]{:S(2)}) async-start(), calls=%async_computation.23 | async-start | bytes 9437184 | tf_op jit(solution)/shard_map/reduce_scatter | solution.py:220
  621.0 246.6 %reduce-scatter.25.cloned.1.call-start = ((), (), s32[]{:S(2)}) async-start(), calls=%async_computation.21 | async-start | bytes 2359296 | tf_op jit(solution)/shard_map/reduce_scatter | solution.py:214
  668.8 4.8 copy-start.17
  668.8 4.8 copy-start.19
  668.8 235.5 %reduce-scatter.19.cloned.1.call-start = ((), (), s32[]{:S(2)}) async-start(), calls=%async_computation.18 | async-start | bytes 2359296 | tf_op jit(solution)/shard_map/reduce_scatter | solution.py:205
  758.1 4.6 copy-start.7
  781.6 159.5 %reduce-scatter.23.cloned.1.call-start = ((), (), s32[]{:S(2)}) async-start(), calls=%async_computation.20 | async-start | bytes 2359296 | tf_op jit(solution)/shard_map/reduce_scatter | solution.py:211
  789.8 188.0 %reduce-scatter.21.cloned.1.call-start = ((), (), s32[]{:S(2)}) async-start(), calls=%async_computation.19 | async-start | bytes 2359296 | tf_op jit(solution)/shard_map/reduce_scatter | solution.py:208
  798.0 251.6 %reduce-scatter.17.cloned.1.call-start = ((), (), s32[]{:S(2)}) async-start(), calls=%async_computation.17 | async-start | bytes 7864320 | tf_op jit(solution)/shard_map/reduce_scatter | solution.py:180
  798.3 10.2 copy-start.15
  798.3 10.2 copy-start.33
  833.6 215.9 %copy-start.21 = (f32[2048]{0:T(1024)S(1)}, f32[2048]{0:T(1024)}, u32[]{:S(2)}) copy-start(f32[2048]{0:T(1024)} %param.23) | copy-start | bytes 24580
  833.6 215.9 %copy-start.23 = (f32[384]{0:T(512)S(1)}, f32[384]{0:T(512)}, u32[]{:S(2)}) copy-start(f32[384]{0:T(512)} %copy-done.22) | copy-start | bytes 4612
  836.4 216.0 %copy-start.31 = (f32[384]{0:T(512)S(1)}, f32[384]{0:T(512)}, u32[]{:S(2)}) copy-start(f32[384]{0:T(512)} %copy-done.30) | copy-start | bytes 4612
  836.4 216.0 %copy-start.26 = (f32[384]{0:T(512)S(1)}, f32[384]{0:T(512)}, u32[]{:S(2)}) copy-start(f32[384]{0:T(512)} %copy-done.25) | copy-start | bytes 4612
  979.6 74.4 %copy-start.27 = (f32[2048]{0:T(1024)S(1)}, f32[2048]{0:T(1024)}, u32[]{:S(2)}) copy-start(f32[2048]{0:T(1024)} %get-tuple-element.141) | copy-start | bytes 24580
  979.6 113.9 %copy-start.29 = (f32[384]{0:T(512)S(1)}, f32[384]{0:T(512)}, u32[]{:S(2)}) copy-start(f32[384]{0:T(512)} %copy-done.28) | copy-start | bytes 4612
  (22 other events, 65.9 us)
Sparse Core Ops, SparseCore 0:
  14.1 72.8 all-gather.4
  163.2 70.2 reduce-scatter.10
  235.3 70.1 all-gather.8
  307.7 70.1 all-gather.6
  426.8 70.1 reduce-scatter.14
  499.8 70.1 reduce-scatter.12
  579.0 70.1 all-gather.10
  651.4 89.5 reduce-scatter.26
  743.4 87.9 reduce-scatter.28
  833.5 34.0 reduce-scatter.24
  870.0 34.3 reduce-scatter.18
  906.5 34.5 reduce-scatter.22
  943.4 34.3 reduce-scatter.20
  980.6 68.8 reduce-scatter.16
where the time goes:
time: 1110 us
  waiting for transfers between devices  616 us (55%)
  matrix products  285 us (26%)
  local copies, waits for them, and re-layouts  78.1 us (7%)
  other arithmetic  71.6 us (6%)
  blocking collectives  39.5 us (4%)
  between operations  14.6 us (1%)
    all_gather x1, waiting for transfers between devices, local(): lax.all_gather(normed_attn.astype(jnp.bfloat16), 'mp', axis=0, tiled=True)  73 us
    reduce_scatter x1, waiting for transfers between devices, local(): lax.psum_scatter(attn_input_back(queries_grad, keys_grad, values_grad, qu...  70 us
    reduce_scatter x1, waiting for transfers between devices, local(): lax.psum_scatter(rows_times(context_flat, out_weight).astype(jnp.bfloat16...  69.6 us
    reduce_scatter x1, waiting for transfers between devices, local(): lax.psum_scatter(rows_times(hidden, down_weight).astype(jnp.bfloat16), 'm...  68.7 us
    all_gather x1, waiting for transfers between devices, local(): cotangent_all = lax.all_gather(out_cotangent, 'mp', axis=0, tiled=True)  66.6 us
    all_gather x1, waiting for transfers between devices, local(): lax.all_gather(normed_mlp.astype(jnp.bfloat16), 'mp', axis=0, tiled=True)  53.4 us
    dot_general x4, matrix products, rows_times_back(): lax.dot_general(left_rows, right_matrix, (((1,), (1,)), ((), ())), prefer...  51.6 us
    reduce_scatter x1, waiting for transfers between devices, local(): lax.psum_scatter(rows_times_back(pre_grad, up_weight).astype(jnp.bfloat16...  49.7 us
  transfers between devices with their start and end apart: 14, of which 12 were waited for; matrix products, arithmetic and copies ran while one was open for 25% of the time, Pallas kernels for 0%

commit v1 on v0

--- a/solution.py
+++ b/solution.py
@@ -7,6 +7,24 @@
 HEAD_DIM = 128
 epsilon = 1e-05
 masked_score = -1e30
+
+
+def in_order(tiles, dim):
+    tiles = jnp.moveaxis(tiles, 0, dim)
+    dims = tiles.shape
+    return tiles.reshape(*dims[:dim], dims[dim] * dims[dim + 1], *dims[dim + 2 :])
+
+
+def grow_blocks(x, axis):
+    size = lax.axis_size(axis)
+    parts = x[None]
+    for level in range(size.bit_length() - 1):
+        stride = 1 << level
+        received = lax.ppermute(parts, axis, [(i, i ^ stride) for i in range(size)])
+        both = jnp.stack([parts, received])
+        upper = lax.axis_index(axis) >> level & 1
+        parts = jnp.where(upper == 0, both, both[::-1]).reshape(-1, *x.shape)
+    return parts
 
 
 def norm_rows(values, gain):
@@ -153,7 +171,8 @@
     ).astype(jnp.float32)
     middle_back, mlp_gain_grad = mlp_norm_back(normed_mlp_grad)
     middle_grad = out_cotangent.astype(jnp.float32) + middle_back
-    middle_all_grad = lax.all_gather(middle_grad.astype(jnp.bfloat16), "mp", axis=0, tiled=True)
+    x = middle_grad.astype(jnp.bfloat16)
+    middle_all_grad = in_order(grow_blocks(x, "mp"), 0)
     out_weight_grad = jnp.einsum(
         "rc,rd->cd", context_flat, middle_all_grad, preferred_element_type=jnp.float32
     )

time: 1110 us -> 1070 us (0.964)
  waiting for transfers between devices: 616 us -> 558 us
  other arithmetic: 71.6 us -> 85.1 us
    ppermute x0 -> x2, waiting for transfers between devices: none -> 100 us  [grow_blocks(): received = lax.ppermute(parts, axis, [(i, i ^ stride) for i in range(size)])]
    reduce_scatter x1, waiting for transfers between devices: 49.7 us -> 6.65 us  [local(): lax.psum_scatter(rows_times_back(pre_grad, up_weight).astype(jnp.bfloat16...]
    reduce_scatter x1, waiting for transfers between devices: 34.9 us -> 0.01 us  [local(): lax.psum_scatter(query_weight_grad.astype(jnp.bfloat16), 'dp', scatter_di...]
    reduce_scatter x1, waiting for transfers between devices: 31.3 us -> 0.01 us  [local(): lax.psum_scatter(out_weight_grad.astype(jnp.bfloat16), 'dp', scatter_dime...]
    all_gather x1 -> x0, waiting for transfers between devices: 28 us -> none  [local(): lax.all_gather(middle_grad.astype(jnp.bfloat16), 'mp', axis=0, tiled=True)]
    reduce_scatter x1, waiting for transfers between devices: 34.9 us -> 14.8 us  [local(): lax.psum_scatter(value_weight_grad.astype(jnp.bfloat16), 'dp', scatter_di...]
    another operation x0 -> x4, other arithmetic: none -> 11.8 us  [grow_blocks(): both = jnp.stack([parts, received])]
  transfers between devices with their start and end apart: 14 -> 15, of which waited for: 12 -> 11; matrix products, arithmetic and copies ran while one was open for 25% -> 28% of each run, Pallas kernels for 0% -> 0%
where the time goes in v1:
time: 1070 us; the launch traced here: 1060 us
  waiting for transfers between devices  558 us (52%)
  matrix products  282 us (26%)
  other arithmetic  85.1 us (8%)
  local copies, waits for them, and re-layouts  80.1 us (7%)
  blocking collectives  39.5 us (4%)
  between operations  14.6 us (1%)
    ppermute x2, waiting for transfers between devices, grow_blocks(): received = lax.ppermute(parts, axis, [(i, i ^ stride) for i in range(size)])  100 us
    all_gather x1, waiting for transfers between devices, local(): lax.all_gather(normed_attn.astype(jnp.bfloat16), 'mp', axis=0, tiled=True)  73 us
    reduce_scatter x1, waiting for transfers between devices, local(): lax.psum_scatter(attn_input_back(queries_grad, keys_grad, values_grad, qu...  70 us
    reduce_scatter x1, waiting for transfers between devices, local(): lax.psum_scatter(rows_times(context_flat, out_weight).astype(jnp.bfloat16...  69.6 us
    reduce_scatter x1, waiting for transfers between devices, local(): lax.psum_scatter(rows_times(hidden, down_weight).astype(jnp.bfloat16), 'm...  68.7 us
    all_gather x1, waiting for transfers between devices, local(): cotangent_all = lax.all_gather(out_cotangent, 'mp', axis=0, tiled=True)  65.4 us
    all_gather x1, waiting for transfers between devices, local(): lax.all_gather(normed_mlp.astype(jnp.bfloat16), 'mp', axis=0, tiled=True)  53.4 us
    dot_general x4, matrix products, rows_times_back(): lax.dot_general(left_rows, right_matrix, (((1,), (1,)), ((), ())), prefer...  51.5 us
  transfers between devices with their start and end apart: 15, of which 11 were waited for; matrix products, arithmetic and copies ran while one was open for 28% of the time, Pallas kernels for 0%

profile of v1, /device:TPU:0, one launch (start us, length us, event | category | flops | bytes accessed | tf_op | source)
XLA Modules:
  0.0 1063.2 jit_solution(14198173460387415344)
XLA Ops:
  14.0 73.0 %all-gather.4.cloned.1.call-done = bf16[1536,2048]{1,0:T(8,128)(2,1)} async-done(((bf16[384,2048]{1,0:T(8,128)(2,1)}), bf16[1536,2048]{1,0:T(8,128)(2,1)}) %all-gather.4.cloned.1.call-update) | async-done | bytes 6291472 | tf_op jit(solution)/shard_map/all_gather | solution.py:124
  87.0 8.0 convolution_convert_fusion.11
  101.6 7.3 fusion.63
  115.3 7.3 convolution_convert_fusion.12
  127.7 28.2 %while.26 = (s32[]{:T(128)}, bf16[2,768,4,128]{3,2,1,0:T(4,128)(2,1)}, f32[2,4,768]{2,1,0:T(4,128)S(1)}, bf16[2,768,4,128]{3,2,1,0:T(4,128)(2,1)}, s32[2,768]{1,...) while((s32[]{:T(128)}, ...), condition=%wide.region_5.6_spmd, body=%wide.region_2.5_spmd.sunk | while | flops 1231352832 | bytes 43362440 | solution.py:137
  163.8 69.6 %reduce-scatter.11.cloned.1.call-done = bf16[384,2048]{1,0:T(8,128)(2,1)} async-done(((bf16[1536,2048]{1,0:T(8,128)(2,1)}), bf16[384,2048]{1,0:T(8,128)(2,1)}) %reduce-scatter.11.cloned.1.call-update) | async-done | bytes 1572880 | tf_op jit(solution)/shard_map/reduce_scatter | solution.py:139
  240.0 65.4 %all-gather.8.cloned.1.call-done = bf16[1536,2048]{1,0:T(8,128)(2,1)} async-done(((bf16[384,2048]{1,0:T(8,128)(2,1)}), bf16[1536,2048]{1,0:T(8,128)(2,1)}) %all-gather.8.cloned.1.call-update) | async-done | bytes 6291472 | tf_op jit(solution)/shard_map/all_gather | solution.py:155
  305.4 19.1 %fusion.91 = f32[1536,2048]{1,0:T(8,128)} fusion(bf16[1536,2048]{1,0:T(8,128)(2,1)} %all-gather.8.cloned.1.call-done, bf16[2048,2048]{1,0:T(8,128)(2,1)} %param.22), kind=kOutput, calls=%fused_computation.152 | convolution fusion | flops 12884901888 | bytes 27262976 | tf_op jit(solution)/shard_map/dot_general | solution.py:159
  324.5 53.4 %all-gather.6.cloned.1.call-done = bf16[1536,2048]{1,0:T(8,128)(2,1)} async-done(((bf16[384,2048]{1,0:T(8,128)(2,1)}), bf16[1536,2048]{1,0:T(8,128)(2,1)}) %all-gather.6.cloned.1.call-update) | async-done | bytes 6291472 | tf_op jit(solution)/shard_map/all_gather | solution.py:147
  377.9 29.6 %fusion.48 = (bf16[1536,2048]{1,0:T(8,128)(2,1)}, f32[1536,2048]{1,0:T(8,128)}) fusion(f32[1536,2048]{1,0:T(8,128)} %fusion.91, bf16[1536,2048]{1,0:T(8,128)(2,1)} %all-gather.6.cloned.1.call-done, bf16[2048,2048]{1,0:T(8,128)(2,1)} %param.21), kind=kOutput, calls=%fused_computation.68 | convolution fusion | flops 12947816448 | bytes 46137344 | tf_op jit(solution)/shard_map/dot_general | solution.py:148
  407.6 19.1 %convolution_convert_fusion.4 = bf16[1536,2048]{1,0:T(8,128)(2,1)} fusion(bf16[1536,2048]{1,0:T(8,128)(2,1)} %get-tuple-element.192, bf16[2048,2048]{1,0:T(8,128)(2,1)} %param.21), kind=kOutput, calls=%fused_computation.74 | convolution fusion | flops 12888047616 | bytes 20971520 | tf_op jit(solution)/shard_map/dot_general | solution.py:51
  426.8 20.5 %convolution_convert_fusion.5 = bf16[1536,2048]{1,0:T(8,128)(2,1)} fusion(bf16[2048,2048]{1,0:T(8,128)(2,1)} %param.22, f32[1536,2048]{1,0:T(8,128)} %get-tuple-element.193), kind=kOutput, calls=%fused_computation.75 | convolution fusion | flops 12916359168 | bytes 27262976 | tf_op jit(solution)/shard_map/dot_general | solution.py:47
  447.4 20.0 %convolution_convert_fusion.3 = bf16[2048,2048]{1,0:T(8,128)(2,1)} fusion(bf16[1536,2048]{1,0:T(8,128)(2,1)} %all-gather.6.cloned.1.call-done, bf16[1536,2048]{1,0:T(8,128)(2,1)} %get-tuple-element.192), kind=kOutput, calls=%fused_computation.73 | convolution fusion | flops 12889096192 | bytes 20971520 | tf_op jit(solution)/shard_map/rd,rf->df/dot_general | solution.py:163
  467.4 22.6 %convolution_convert_fusion.2 = bf16[2048,2048]{1,0:T(8,128)(2,1)} fusion(bf16[1536,2048]{1,0:T(8,128)(2,1)} %all-gather.8.cloned.1.call-done, f32[1536,2048]{1,0:T(8,128)} %get-tuple-element.193), kind=kOutput, calls=%fused_computation.72 | convolution fusion | flops 12917407744 | bytes 27262976 | tf_op jit(solution)/shard_map/rf,rd->fd/dot_general | solution.py:156
  501.5 68.7 %reduce-scatter.13.cloned.1.call-done = bf16[384,2048]{1,0:T(8,128)(2,1)} async-done(((bf16[1536,2048]{1,0:T(8,128)(2,1)}), bf16[384,2048]{1,0:T(8,128)(2,1)}) %reduce-scatter.13.cloned.1.call-update) | async-done | bytes 1572880 | tf_op jit(solution)/shard_map/reduce_scatter | solution.py:151
  582.0 32.3 %collective-permute-done = bf16[1,384,2048]{2,1,0:T(8,128)(2,1)} collective-permute-done((bf16[1,384,2048]{2,1,0:T(8,128)(2,1)}, bf16[1,384,2048]{2,1,0:T(8,128)(2,1)}, u32[]{:S(2)}, u32[]{:S(2)}) %collective-permute-start) | collective-permute-done | bytes 1572896 | tf_op jit(solution)/shard_map/ppermute | solution.py:23
  621.2 68.0 %collective-permute-done.1 = bf16[2,384,2048]{2,1,0:T(8,128)(2,1)} collective-permute-done((bf16[2,384,2048]{2,1,0:T(8,128)(2,1)}, bf16[2,384,2048]{2,1,0:T(8,128)(2,1)}, u32[]{:S(2)}, u32[]{:S(2)}) %collective-permute-start.1) | collective-permute-done | bytes 3145760 | tf_op jit(solution)/shard_map/ppermute | solution.py:23
  706.4 8.2 convolution_convert_fusion.7
  719.3 98.4 %while.27 = (s32[]{:T(128)}, bf16[2,768,4,128]{3,2,1,0:T(4,128)(2,1)}, bf16[2,768,4,128]{3,2,1,0:T(4,128)(2,1)}, bf16[2,768,4,128]{3,2,1,0:T(4,128)(2,1)}, bf16[...) while((s32[]{:T(128)}, ...), condition=%wide.region_15.16_spmd, body=%wide.region_13.15_spmd.sunk | while | flops 3051156480 | bytes 169179440 | solution.py:182
  734.6 8.1 multiply_reduce_fusion.3
  742.7 10.9 %multiply_convert_fusion.7 = bf16[4,768,768]{1,2,0:T(8,128)(2,1)} fusion(f32[4,768,768]{1,2,0:T(8,128)} %get-tuple-element.306, f32[4,768,768]{1,2,0:T(8,128)} %copy-done.1, f32[4,768]{1,0:T(4,128)S(1)} %get-tuple-element.307, f32[4,768]{1,0:T(4,128)S(1)} %dynamic-slice_bitcast_fusion.2, pred[768,768]{0,1:T(8,128)(4,1)S(1)} %fusion.150), kind=kLoop, calls=%fused_computation.21.clone.1 | loop fusion | flops 11796480 | bytes 24207360 | tf_op jit(solution)/shard_map/while/body/eval_jaxpr/convert_element_type | solution.py:91
  783.8 8.0 multiply_reduce_fusion.3
  791.8 10.7 %multiply_convert_fusion.7 = bf16[4,768,768]{1,2,0:T(8,128)(2,1)} fusion(f32[4,768,768]{1,2,0:T(8,128)} %get-tuple-element.306, f32[4,768,768]{1,2,0:T(8,128)} %copy-done.1, f32[4,768]{1,0:T(4,128)S(1)} %get-tuple-element.307, f32[4,768]{1,0:T(4,128)S(1)} %dynamic-slice_bitcast_fusion.2, pred[768,768]{0,1:T(8,128)(4,1)S(1)} %fusion.150), kind=kLoop, calls=%fused_computation.21.clone.1 | loop fusion | flops 11796480 | bytes 24207360 | tf_op jit(solution)/shard_map/while/body/eval_jaxpr/convert_element_type | solution.py:91
  817.7 8.0 multiply_convert_fusion.2
  825.8 8.0 convolution_convert_fusion.8
  833.9 8.1 convolution_convert_fusion.9
  842.3 10.2 fusion.74
  859.0 15.7 %add_convert_fusion = bf16[1536,2048]{1,0:T(8,128)(2,1)} fusion(f32[1536,2048]{1,0:T(8,128)} %fusion.71, f32[1536,2048]{1,0:T(8,128)} %fusion.74, bf16[2048,512]{1,0:T(8,128)(2,1)} %param.17, bf16[192,8,4,128]{3,2,1,0:T(4,128)(2,1)} %bitcast.158), kind=kOutput, calls=%fused_computation.69 | convolution fusion | flops 3233808384 | bytes 35127296 | tf_op jit(solution)/shard_map/dot_general | solution.py:51
  883.9 14.8 %reduce-scatter.23.cloned.1.call-done = bf16[256,512]{1,0:T(8,128)(2,1)} async-done(((bf16[2048,512]{1,0:T(8,128)(2,1)}), bf16[256,512]{1,0:T(8,128)(2,1)}) %reduce-scatter.23.cloned.1.call-update) | async-done | bytes 262160 | tf_op jit(solution)/shard_map/reduce_scatter | solution.py:230
  900.5 34.9 %reduce-scatter.21.cloned.1.call-done = bf16[256,512]{1,0:T(8,128)(2,1)} async-done(((bf16[2048,512]{1,0:T(8,128)(2,1)}), bf16[256,512]{1,0:T(8,128)(2,1)}) %reduce-scatter.21.cloned.1.call-update) | async-done | bytes 262160 | tf_op jit(solution)/shard_map/reduce_scatter | solution.py:227
  937.2 70.0 %reduce-scatter.17.cloned.1.call-done = bf16[384,2048]{1,0:T(8,128)(2,1)} async-done(((bf16[1536,2048]{1,0:T(8,128)(2,1)}), bf16[384,2048]{1,0:T(8,128)(2,1)}) %reduce-scatter.17.cloned.1.call-update) | async-done | bytes 1572880 | tf_op jit(solution)/shard_map/reduce_scatter | solution.py:199
  1011.6 39.5 %all-reduce = (f32[2048]{0:T(1024)}, f32[2048]{0:T(1024)}) all-reduce(f32[2048]{0:T(1024)S(1)} %get-tuple-element.143, f32[2048]{0:T(1024)S(1)} %copy-done.33), channel_id=1, replica_groups=mesh['dp'=8,'mp'=4] {'dp','mp'}, use_global_device_ids=true, to_apply=%region_26.27 | all-reduce | flops 4096 | bytes 32768 | tf_op jit(solution)/shard_map/psum | solution.py:215
  (222 shorter events, 209.1 us)
Async XLA Ops:
  7.2 148.7 %copy-start = (bf16[512,2048]{1,0:T(8,128)(2,1)S(1)}, bf16[512,2048]{1,0:T(8,128)(2,1)}, u32[]{:S(2)}) copy-start(bf16[512,2048]{1,0:T(8,128)(2,1)} %param.20) | copy-start | bytes 6291460
  7.2 5.1 copy-start.21
  7.2 79.8 %all-gather.4.cloned.1.call-start = ((), (), s32[]{:S(2)}) async-start(), calls=%async_computation.10 | async-start | bytes 7864320 | tf_op jit(solution)/shard_map/all_gather | solution.py:124
  14.0 219.4 %reduce-scatter.11.cloned.1.call-start = ((), (), s32[]{:S(2)}) async-start(), calls=%async_computation.11 | async-start | bytes 7864320 | tf_op jit(solution)/shard_map/reduce_scatter | solution.py:139
  155.8 7.2 copy-start.17
  163.0 142.4 %all-gather.8.cloned.1.call-start = ((), (), s32[]{:S(2)}) async-start(), calls=%async_computation.14 | async-start | bytes 7864320 | tf_op jit(solution)/shard_map/all_gather | solution.py:155
  163.1 75.0 %copy-start.25 = (f32[2048]{0:T(1024)S(1)}, f32[2048]{0:T(1024)}, u32[]{:S(2)}) copy-start(f32[2048]{0:T(1024)} %param.24) | copy-start | bytes 24580
  163.8 214.1 %all-gather.6.cloned.1.call-start = ((), (), s32[]{:S(2)}) async-start(), calls=%async_computation.12 | async-start | bytes 7864320 | tf_op jit(solution)/shard_map/all_gather | solution.py:147
  240.0 257.1 %reduce-scatter.15.cloned.1.call-start = ((), (), s32[]{:S(2)}) async-start(), calls=%async_computation.15 | async-start | bytes 7864320 | tf_op jit(solution)/shard_map/reduce_scatter | solution.py:166
  426.7 143.5 %reduce-scatter.13.cloned.1.call-start = ((), (), s32[]{:S(2)}) async-start(), calls=%async_computation.13 | async-start | bytes 7864320 | tf_op jit(solution)/shard_map/reduce_scatter | solution.py:151
  447.3 427.4 %reduce-scatter.27.cloned.1.call-start = ((), (), s32[]{:S(2)}) async-start(), calls=%async_computation.21 | async-start | bytes 9437184 | tf_op jit(solution)/shard_map/reduce_scatter | solution.py:236
  467.4 410.2 %reduce-scatter.29.cloned.1.call-start = ((), (), s32[]{:S(2)}) async-start(), calls=%async_computation.22 | async-start | bytes 9437184 | tf_op jit(solution)/shard_map/reduce_scatter | solution.py:239
  490.1 7.0 copy-start.26
  490.1 7.0 copy-start.28
  490.1 7.0 copy-start.35
  490.1 11.4 %copy-start.39 = (f32[384]{0:T(512)S(1)}, f32[384]{0:T(512)}, u32[]{:S(2)}) copy-start(f32[384]{0:T(512)} %copy-done.38) | copy-start | bytes 4612
  490.1 390.2 %reduce-scatter.25.cloned.1.call-start = ((), (), s32[]{:S(2)}) async-start(), calls=%async_computation.20 | async-start | bytes 2359296 | tf_op jit(solution)/shard_map/reduce_scatter | solution.py:233
  570.2 5.5 copy-start.11
  577.9 36.5 %collective-permute-start = (bf16[1,384,2048]{2,1,0:T(8,128)(2,1)}, bf16[1,384,2048]{2,1,0:T(8,128)(2,1)}, u32[]{:S(2)}, u32[]{:S(2)}) collective-permute-start(bf16[1,384,2048]{2,1,0:T(8,128)(2,1)} %fusion.121), channel_id=1, source_target_pairs={{0,1},{1,0},{2,3},{3,2},{4,5},{5,4},{6,7},{7,6},{8,9},{9,8},{10,11... | collective-permute-start | bytes 4718600 | tf_op jit(solution)/shard_map/ppermute | solution.py:23
  619.8 69.3 %collective-permute-start.1 = (bf16[2,384,2048]{2,1,0:T(8,128)(2,1)}, bf16[2,384,2048]{2,1,0:T(8,128)(2,1)}, u32[]{:S(2)}, u32[]{:S(2)}) collective-permute-start(bf16[2,384,2048]{2,1,0:T(8,128)(2,1)} %get-tuple-element.190), channel_id=1, source_target_pairs={{0,2},{1,3},{2,0},{3,1},{4,6},{5,7},{6,4},{7,5},{8,10},{9,11},{10,... | collective-permute-start | bytes 9437192 | tf_op jit(solution)/shard_map/ppermute | solution.py:23
  714.6 167.5 %reduce-scatter.19.cloned.1.call-start = ((), (), s32[]{:S(2)}) async-start(), calls=%async_computation.17 | async-start | bytes 2359296 | tf_op jit(solution)/shard_map/reduce_scatter | solution.py:224
  825.8 72.9 %reduce-scatter.23.cloned.1.call-start = ((), (), s32[]{:S(2)}) async-start(), calls=%async_computation.19 | async-start | bytes 2359296 | tf_op jit(solution)/shard_map/reduce_scatter | solution.py:230
  833.8 101.5 %reduce-scatter.21.cloned.1.call-start = ((), (), s32[]{:S(2)}) async-start(), calls=%async_computation.18 | async-start | bytes 2359296 | tf_op jit(solution)/shard_map/reduce_scatter | solution.py:227
  842.0 165.1 %reduce-scatter.17.cloned.1.call-start = ((), (), s32[]{:S(2)}) async-start(), calls=%async_computation.16 | async-start | bytes 7864320 | tf_op jit(solution)/shard_map/reduce_scatter | solution.py:199
  842.3 10.2 copy-start.16
  842.3 10.2 copy-start.41
  877.5 129.6 %copy-start.22 = (f32[2048]{0:T(1024)S(1)}, f32[2048]{0:T(1024)}, u32[]{:S(2)}) copy-start(f32[2048]{0:T(1024)} %param.23) | copy-start | bytes 24580
  877.5 129.6 %copy-start.24 = (f32[384]{0:T(512)S(1)}, f32[384]{0:T(512)}, u32[]{:S(2)}) copy-start(f32[384]{0:T(512)} %copy-done.23) | copy-start | bytes 4612
  880.3 129.7 %copy-start.37 = (f32[384]{0:T(512)S(1)}, f32[384]{0:T(512)}, u32[]{:S(2)}) copy-start(f32[384]{0:T(512)} %copy-done.36) | copy-start | bytes 4612
  880.3 129.7 %copy-start.30 = (f32[384]{0:T(512)S(1)}, f32[384]{0:T(512)}, u32[]{:S(2)}) copy-start(f32[384]{0:T(512)} %copy-done.29) | copy-start | bytes 4612
  937.2 74.4 %copy-start.33 = (f32[2048]{0:T(1024)S(1)}, f32[2048]{0:T(1024)}, u32[]{:S(2)}) copy-start(f32[2048]{0:T(1024)} %get-tuple-element.141) | copy-start | bytes 24580
  937.2 113.9 %copy-start.32 = (f32[384]{0:T(512)S(1)}, f32[384]{0:T(512)}, u32[]{:S(2)}) copy-start(f32[384]{0:T(512)} %copy-done.31) | copy-start | bytes 4612
  (31 other events, 97.1 us)
Sparse Core Ops, SparseCore 0:
  14.1 72.8 all-gather.3
  163.2 70.2 reduce-scatter.10
  235.3 70.1 all-gather.7
  307.7 70.1 all-gather.5
  426.9 70.2 reduce-scatter.14
  499.9 70.2 reduce-scatter.12
  572.5 89.5 reduce-scatter.26
  664.4 87.9 reduce-scatter.28
  754.7 34.1 reduce-scatter.24
  825.9 35.9 reduce-scatter.18
  864.1 34.4 reduce-scatter.22
  900.8 34.5 reduce-scatter.20
  938.3 68.7 reduce-scatter.16
